TPU v7x, 128 devices: a whole 4x4x4 slice. The times are simulated.
128 devices in a mesh: gx: 8 (over x_lo, z), gy: 16 (over x_hi, y, core).
Axes of the slice: x: 4 (x_hi: 2, x_lo: 2; x = x_hi * 2 + x_lo), y: 4, z: 4, core: 2. Of those that a mesh axis runs over, the one named last changes fastest.
Arguments:
- scalars: float32 [4, 64, 128, 2048], P(None, None, 'gx', 'gy'), may hold values from -6 to 6
- winds: float32 [2, 64, 128, 2048], P(None, None, 'gx', 'gy'), may hold values from -0.6 to 0.6
- map_factor: float32 [128, 2048], P('gx', 'gy'), may hold values from 0.7 to 1.3
- urban_counts: int32 [128], P(('gx', 'gy')), may hold values from 256 to 1024, as said below
- urban_cols: int32 [131072], P(('gx', 'gy')), may hold values from 0 to 2047, as said below
- street_class: int32 [131072], P(('gx', 'gy')), may hold values from 0 to 9
- area_table: float32 [10, 10], replicated, may hold values from 0.2 to 1
- wall_temp: float32 [10, 131072], P(None, ('gx', 'gy')), may hold values from -6 to 6
- indoor_temp: float32 [131072], P(('gx', 'gy')), may hold values from -6 to 6
Outputs:
- scalars_out: float32 [4, 64, 128, 2048], P(None, None, 'gx', 'gy')
- wall_out: float32 [10, 131072], P(None, ('gx', 'gy'))
- indoor_out: float32 [131072], P(('gx', 'gy'))
Inputs may be any that keep to these rules, and one draw needn't show every extreme that they name: `urban_counts`: some tile has exactly 1024 live urban columns. `urban_cols`: the 1024 entries of each tile are distinct cells of that tile, numbered x * 128 + y within it.
All inputs are finite; a program needn't handle non-finite values.
Results may differ from a plain program's by a relative error of at most 0.000056.
Values sent between devices are 32-bit elements; how exact they have to be, the bound alone decides.
A program may use at most 192 MiB of HBM per device.

v0:
```python
import jax
import jax.numpy as jnp
from jax import lax
from jax.experimental import pallas as pl
from jax.experimental.pallas import tpu as pltpu
from jax.sharding import PartitionSpec as P

MESH = pl.DeviceIdType.MESH
UL = 10
NWL = 10
LOW = 16

heat_coef = 0.5
wall_coef = 0.05
conduct = 0.3
inner_coef = 0.2
room_coef = 0.1
flux_coef = 0.5

CX = 16
LANES = 128
NSC = 4
LEV = 64
ROWS = 8
CHUNKS = LEV // ROWS
STRIDE = LEV + ROWS
H = 3
EDGE_X = (0, 1, 2, 13, 14, 15)
INNER_X = tuple(range(3, 13))


def roll(value, shift):
    return pltpu.roll(value, shift % LANES, 1)


def split(value):
    high = value.astype(jnp.bfloat16)
    return high, (value - high.astype(jnp.float32)).astype(jnp.bfloat16)


def fill_stencil(stencil):
    row = lax.broadcasted_iota(jnp.int32, (LANES, LANES), 0)
    column = lax.broadcasted_iota(jnp.int32, (LANES, LANES), 1)
    for block in range(4):
        offset = row - column + (2 if block < 2 else 3)
        weights = (1.0, -8.0, 37.0, 37.0, -8.0, 1.0) if block % 2 == 0 else (-1.0, 5.0, -10.0, 10.0, -5.0, 1.0)
        band = jnp.zeros((LANES, LANES), jnp.float32)
        for at, weight in enumerate(weights):
            band = jnp.where(offset == at, weight, band)
        band = band.astype(jnp.bfloat16)
        for part in range(2):
            stencil[pl.ds(part * LANES, LANES), pl.ds(block * LANES, LANES)] = band


def urban(counts, cols, classes, table, wall, indoor, out, wall_out, indoor_out, body, heat_pad):
    slots = cols.shape[1]
    column = cols[...]
    col_x = column // LANES
    col_y = column % LANES
    live = lax.broadcasted_iota(jnp.int32, (1, slots), 1) < counts[0]
    onehot = (lax.broadcasted_iota(jnp.int32, (LANES, slots), 0) == col_y).astype(jnp.float32)
    ncls = table.shape[0]
    picked = (lax.broadcasted_iota(jnp.int32, (ncls, slots), 0) == classes[...]).astype(jnp.float32)
    areas = lax.dot_general(
        table[...], picked, (((0,), (0,)), ((), ())), precision=lax.Precision.HIGHEST, preferred_element_type=jnp.float32
    )
    lowest = out[:, 0, pl.ds(0, LOW), :]
    gathered = jnp.dot(
        lowest.reshape(CX * LOW, LANES), onehot, precision=lax.Precision.HIGHEST, preferred_element_type=jnp.float32
    ).reshape(CX, LOW, slots)
    air = jnp.zeros((LOW, slots), jnp.float32)
    for x in range(CX):
        air = jnp.where(col_x == x, gathered[x], air)
    walls = wall[...]
    room = indoor[...]
    top = walls[0:1]
    heat = heat_coef * areas * (top - air[:UL])
    first = top - wall_coef * jnp.sum(heat, axis=0, keepdims=True) + conduct * (walls[1:2] - top)
    middle = walls[1:-1] + conduct * (walls[:-2] - 2.0 * walls[1:-1] + walls[2:])
    bottom = walls[NWL - 1 : NWL]
    last = bottom + conduct * (walls[NWL - 2 : NWL - 1] - bottom) + inner_coef * (room - bottom)
    wall_out[0:1] = jnp.where(live, first, top)
    wall_out[1 : NWL - 1] = jnp.where(live, middle, walls[1:-1])
    wall_out[NWL - 1 : NWL] = jnp.where(live, last, bottom)
    indoor_out[...] = jnp.where(live, room + room_coef * (bottom - room), room)
    heat_pad[...] = jnp.zeros_like(heat_pad)
    heat_pad[0:UL] = jnp.where(live, flux_coef * heat, 0.0)
    padded = heat_pad[...]
    for x in range(CX):
        body[x] = jnp.where(col_x == x, padded, 0.0)
    spread = lax.dot_general(
        body[...].reshape(CX * LOW, slots), onehot, (((1,), (1,)), ((), ())),
        precision=lax.Precision.HIGHEST, preferred_element_type=jnp.float32,
    )
    out[:, 0, pl.ds(0, LOW), :] = out[:, 0, pl.ds(0, LOW), :] + spread.reshape(CX, LOW, LANES)


def step_kernel(
    scal, wind, mapf, counts, cols, classes, table, wall, indoor, out, wall_out, indoor_out,
    field0, field1, field2, windx, windy, facex, face_r, face_l, edge_weight, square, give_n, give_s, got_s, got_n,
    wpack, wgot, mapbuf, stencil, cells, across,
    load_s, load_w, load_m, sx, rx, sy, ry, swx, rwx, swy, rwy,
    cols_buf, classes_buf, table_buf, wall_buf, indoor_buf, spread_in, heat_pad, load_u,
):
    fields = (field0, field1, field2)
    gx, gy = lax.axis_index("gx"), lax.axis_index("gy")
    nx, ny = lax.axis_size("gx"), lax.axis_size("gy")
    east, west = {"gx": lax.rem(gx + 1, nx)}, {"gx": lax.rem(gx + nx - 1, nx)}
    north, south = {"gy": lax.rem(gy + 1, ny)}, {"gy": lax.rem(gy + ny - 1, ny)}

    barrier = pltpu.get_barrier_semaphore()
    for device in (east, west, north, south):
        pl.semaphore_signal(barrier, inc=1, device_id=device, device_id_type=MESH)

    def load_scalar(s, x):
        return pltpu.make_async_copy(scal.at[s, :, x, :], field0.at[H + x, s, pl.ds(0, LEV), :], load_s.at[s, x])

    def load_wind(which, x):
        target = (windx.at[1 + x] if which == 0 else windy.at[x]).at[pl.ds(0, LEV), :]
        return pltpu.make_async_copy(wind.at[which, :, x, :], target, load_w.at[which, x])

    load_map = pltpu.make_async_copy(mapf, mapbuf, load_m)
    for s in range(NSC):
        for x in EDGE_X:
            load_scalar(s, x).start()
    load_wind(0, 0).start()
    load_wind(0, CX - 1).start()
    for x in range(CX):
        load_wind(1, x).start()
    for s in range(NSC):
        for x in INNER_X:
            load_scalar(s, x).start()
    for x in range(1, CX - 1):
        load_wind(0, x).start()
    load_map.start()
    urban_loads = [
        pltpu.make_async_copy(source, target, load_u.at[n])
        for n, (source, target) in enumerate(
            ((cols, cols_buf), (classes, classes_buf), (table, table_buf), (wall, wall_buf), (indoor, indoor_buf))
        )
    ]
    for copy in urban_loads:
        copy.start()

    def remote(src, dst, send, recv, device):
        return pltpu.make_async_remote_copy(
            src_ref=src, dst_ref=dst, send_sem=send, recv_sem=recv, device_id=device, device_id_type=MESH
        )

    def rows_of(k):
        return pl.ds(pl.multiple_of(k * ROWS, ROWS), ROWS)

    def x_copies(sec, k):
        rows = rows_of(k)
        return (
            remote(fields[sec].at[pl.ds(CX, H), :, rows, :], fields[sec].at[pl.ds(0, H), :, rows, :],
                   sx.at[sec, k, 0], rx.at[sec, k, 0], east),
            remote(fields[sec].at[pl.ds(H, H), :, rows, :], fields[sec].at[pl.ds(CX + H, H), :, rows, :],
                   sx.at[sec, k, 1], rx.at[sec, k, 1], west),
        )

    def y_copies(sec, k):
        return (
            remote(give_n.at[sec, k], got_s.at[sec, k], sy.at[sec, k, 0], ry.at[sec, k, 0], north),
            remote(give_s.at[sec, k], got_n.at[sec, k], sy.at[sec, k, 1], ry.at[sec, k, 1], south),
        )

    wx_copies = (
        remote(windx.at[CX, pl.ds(0, LEV), :], windx.at[0, pl.ds(0, LEV), :], swx.at[0], rwx.at[0], east),
        remote(windx.at[1, pl.ds(0, LEV), :], windx.at[CX + 1, pl.ds(0, LEV), :], swx.at[1], rwx.at[1], west),
    )
    wy_copies = (
        remote(wpack.at[0], wgot.at[0], swy.at[0], rwy.at[0], north),
        remote(wpack.at[1], wgot.at[1], swy.at[1], rwy.at[1], south),
    )

    for s in range(NSC):
        for x in EDGE_X:
            load_scalar(s, x).wait()
    load_wind(0, 0).wait()
    load_wind(0, CX - 1).wait()
    pl.semaphore_wait(barrier, 4)
    for copy in wx_copies:
        copy.start()

    def send_first(k, carry):
        for copy in x_copies(0, k):
            copy.start()
        return carry

    lax.fori_loop(0, CHUNKS, send_first, 0)
    fill_stencil(stencil)

    lane = lax.broadcasted_iota(jnp.int32, (ROWS, LANES), 1)
    slot = lane // 8
    inside = lane % 8
    low = inside < 3

    def pack_send(sec, k, pair, first, second):
        give_n[sec, k, pair] = jnp.where(low, first, roll(second, 3))
        give_s[sec, k, pair] = jnp.where(low, roll(first, -3), second)

    for x in range(CX):
        load_wind(1, x).wait()
    to_n = jnp.zeros((ROWS, LANES), jnp.float32)
    to_s = jnp.zeros((ROWS, LANES), jnp.float32)
    lanes = lax.broadcasted_iota(jnp.int32, (LEV, LANES), 1) // 8
    packed = jnp.zeros((LEV, LANES), jnp.float32)
    for x in range(CX):
        packed = jnp.where(lanes == x, roll(windy[x, pl.ds(0, LEV), :], 8 * x + 3), packed)
    for k in range(CHUNKS):
        piece = packed[k * ROWS : (k + 1) * ROWS]
        to_n = jnp.where(inside == k, roll(piece, k - 2), to_n)
        to_s = jnp.where(inside == k, roll(piece, k - 3), to_s)
    wpack[0] = to_n
    wpack[1] = to_s
    for copy in wy_copies:
        copy.start()

    for s in range(NSC):
        for x in INNER_X:
            load_scalar(s, x).wait()

    many = lax.broadcasted_iota(jnp.int32, (NSC * ROWS, LANES), 1) // 8

    def pack_first(k, carry):
        rows = rows_of(k)
        packed = jnp.zeros((NSC * ROWS, LANES), jnp.float32)
        for x in range(CX):
            value = field0[H + x, :, rows, :].reshape(NSC * ROWS, LANES)
            packed = jnp.where(many == x, roll(value, 8 * x + 3), packed)
        for pair in range(2):
            at = 2 * pair * ROWS
            pack_send(0, k, pair, packed[at : at + ROWS], packed[at + ROWS : at + 2 * ROWS])
        for copy in y_copies(0, k):
            copy.start()
        return carry

    lax.fori_loop(0, CHUNKS, pack_first, 0)

    load_map.wait()
    for x in range(CX):
        factor = jnp.broadcast_to(mapbuf[pl.ds(x, 1), :], (ROWS, LANES))
        minus = factor * factor
        square[0, x] = minus * (1.0 / 3.0)
        square[1, x] = minus * 0.5
        square[2, x] = minus
    for x in range(1, CX - 1):
        load_wind(0, x).wait()
    for copy in wx_copies:
        copy.wait_recv()
    for copy in wy_copies:
        copy.wait_recv()

    from_s = wgot[0]
    from_n = wgot[1]
    half_levels = LEV // 2
    lanes = lax.broadcasted_iota(jnp.int32, (half_levels, LANES), 1)
    slots, within = lanes // 8, lanes % 8
    below = within < 3
    for part in range(2):
        rows = pl.ds(part * half_levels, half_levels)
        for x in range(CX + 1):
            facex[x, rows, :] = (windx[x, rows, :] + windx[x + 1, rows, :]) * (1.0 / 120.0)
        merged = jnp.concatenate(
            [
                jnp.where(low, roll(from_s, 2 - k), roll(from_n, 3 - k))
                for k in range(part * CHUNKS // 2, (part + 1) * CHUNKS // 2)
            ],
            axis=0,
        )
        zero = jnp.zeros((half_levels, LANES), jnp.float32)

        def faces(x, packed):
            left, right = packed
            centre = windy[x, rows, :]
            halo = roll(merged, -(8 * x + 3))
            behind = (roll(jnp.where(lanes == LANES - 1, halo, centre), 1) + centre) * (1.0 / 120.0)
            ahead = (roll(jnp.where(lanes == 0, halo, centre), -1) + centre) * (1.0 / 120.0)
            face_l[x, rows, :] = behind
            face_r[x, rows, :] = ahead
            return (
                jnp.where(slots == x, roll(behind, 8 * x + 3), left),
                jnp.where(slots == x, roll(ahead, 8 * x + 3), right),
            )

        left, right = zero, zero
        for x in range(CX):
            left, right = faces(x, (left, right))
        right_abs, left_abs = jnp.abs(right), jnp.abs(left)
        three = jnp.where(below, right - right_abs, jnp.where(within < 6, -(left + left_abs), zero))
        two = jnp.where(
            (within == 1) | (within == 2),
            (5.0 * right_abs - 8.0 * right) + (left_abs - left),
            jnp.where((within == 3) | (within == 4), (right + right_abs) + (8.0 * left + 5.0 * left_abs), zero),
        )
        one = jnp.where(
            within == 2,
            (37.0 * right - 10.0 * right_abs) + (8.0 * left - 5.0 * left_abs),
            jnp.where(within == 3, -(8.0 * right + 5.0 * right_abs) - (37.0 * left + 10.0 * left_abs), zero),
        )
        edge_weight[0, rows, :] = one
        edge_weight[1, rows, :] = two
        edge_weight[2, rows, :] = three

    size = NSC * ROWS
    half = CX // 2
    edge = (lane < H) | (lane >= LANES - H)

    def section(sec, k, last):
        rows = rows_of(k)
        for part in range(2):
            for x in range(part * half, (part + 1) * half):
                at = pl.ds(x * size, size)
                high, rest = split(fields[sec][H + x, :, rows, :].reshape(size, LANES))
                cells[at, 0:LANES] = high
                cells[at, LANES : 2 * LANES] = rest
            at = pl.ds(part * half * size, half * size)
            across[at, :] = jnp.dot(cells[at, :], stencil[...], preferred_element_type=jnp.float32)
        for pair in range(2):
            from_south, from_north = got_s[sec, k, pair], got_n[sec, k, pair]
            halos = (
                jnp.where(low, from_south, roll(from_north, 3)),
                jnp.where(low, roll(from_south, -3), from_north),
            )
            added = []
            for halo in halos:
                added.append(
                    sum(
                        edge_weight[r - 1, rows, :] * jnp.where(low, roll(halo, -r), roll(halo, r))
                        for r in (1, 2, 3)
                    )
                )
            members = (2 * pair, 2 * pair + 1)
            packs = {s: jnp.zeros((ROWS, LANES), jnp.float32) for s in members}
            q, g, d2, d3, d4, even, flux = ({s: {} for s in members} for _ in range(7))
            for i in range(CX + 2 * H):
                f, x = i - 5, i - 6
                if f >= 0:
                    speed = facex[f, rows, :]
                    speed_abs = jnp.abs(speed)
                if x >= 0:
                    ahead, behind, scale = face_r[x, rows, :], face_l[x, rows, :], square[sec, x]
                    ahead_abs, behind_abs = jnp.abs(ahead), jnp.abs(behind)
                for s in members:
                    q[s][i] = fields[sec][i, s, rows, :]
                    if i >= 1:
                        g[s][i - 1] = q[s][i] - q[s][i - 1]
                    if i >= 2:
                        d2[s][i - 1] = g[s][i - 1] - g[s][i - 2]
                    if i >= 3:
                        d3[s][i - 2] = d2[s][i - 1] - d2[s][i - 2]
                    if i >= 4:
                        d4[s][i - 2] = d3[s][i - 2] - d3[s][i - 3]
                        even[s][i - 2] = (d4[s][i - 2] - 5.0 * d2[s][i - 2]) + 30.0 * q[s][i - 2]
                    if f >= 0:
                        flux[s][f] = speed * (even[s][i - 3] + even[s][i - 2]) - speed_abs * (d4[s][i - 2] - d4[s][i - 3])
                    if x >= 0:
                        at = pl.ds(x * size + s * ROWS, ROWS)
                        total = flux[s][x + 1] - flux[s][x]
                        total += ahead * across[at, 0:LANES] - ahead_abs * across[at, LANES : 2 * LANES]
                        total -= behind * across[at, 2 * LANES : 3 * LANES] - behind_abs * across[at, 3 * LANES : 4 * LANES]
                        total += jnp.where(edge, roll(added[s % 2], -(8 * x + 3)), 0.0)
                        new = (field0[H + x, s, rows, :] if sec else q[s][H + x]) - scale * total
                        if last:
                            out[x, s, rows, :] = new
                        else:
                            fields[sec + 1][H + x, s, rows, :] = new
                            packs[s] = jnp.where(slot == x, roll(new, 8 * x + 3), packs[s])
            if not last:
                pack_send(sec + 1, k, pair, packs[members[0]], packs[members[1]])

    for sec in range(2):

        def early(k, carry, sec=sec):
            for copy in x_copies(sec, k) + y_copies(sec, k):
                copy.wait_recv()
            section(sec, k, False)
            for copy in x_copies(sec + 1, k) + y_copies(sec + 1, k):
                copy.start()
            return carry

        lax.fori_loop(0, CHUNKS, early, 0)

    def late(k, carry):
        for copy in x_copies(2, k) + y_copies(2, k):
            copy.wait_recv()
        section(2, k, True)

        @pl.when(k == LOW // ROWS - 1)
        def _():
            for copy in urban_loads:
                copy.wait()
            urban(counts, cols_buf, classes_buf, table_buf, wall_buf, indoor_buf, out, wall_out, indoor_out, spread_in, heat_pad)

        return carry

    lax.fori_loop(0, CHUNKS, late, 0)

    for copy in wx_copies + wy_copies:
        copy.wait_send()

    def finish(k, carry):
        for sec in range(3):
            for copy in x_copies(sec, k) + y_copies(sec, k):
                copy.wait_send()
        return carry

    lax.fori_loop(0, CHUNKS, finish, 0)


def advance(scalars, winds, map_factor, counts, cols, classes, table, wall, indoor):
    f32, i32 = jnp.float32, jnp.int32
    dma = pltpu.SemaphoreType.DMA
    slots = wall.shape[1]
    vmem = pl.BlockSpec(memory_space=pltpu.VMEM)
    anywhere = pl.BlockSpec(memory_space=pl.ANY)
    grids = (scalars, winds, map_factor)
    columns = (cols.reshape(1, slots), classes.reshape(1, slots), table, wall, indoor.reshape(1, slots))
    operands = [pltpu.with_memory_space_constraint(array, pltpu.HBM) for array in grids + columns]
    operands.insert(len(grids), counts)
    return pl.pallas_call(
        step_kernel,
        out_shape=(
            jax.ShapeDtypeStruct((CX, NSC, LEV, LANES), f32),
            jax.ShapeDtypeStruct((NWL, slots), f32),
            jax.ShapeDtypeStruct((1, slots), f32),
        ),
        in_specs=[anywhere] * 3 + [pl.BlockSpec(memory_space=pltpu.SMEM)] + [anywhere] * 5,
        out_specs=(vmem, vmem, vmem),
        scratch_shapes=[
            pltpu.VMEM((CX + 2 * H, NSC, STRIDE, LANES), f32),
            pltpu.VMEM((CX + 2 * H, NSC, STRIDE, LANES), f32),
            pltpu.VMEM((CX + 2 * H, NSC, STRIDE, LANES), f32),
            pltpu.VMEM((CX + 2, STRIDE, LANES), f32),
            pltpu.VMEM((CX, STRIDE, LANES), f32),
            pltpu.VMEM((CX + 1, STRIDE, LANES), f32),
            pltpu.VMEM((CX, STRIDE, LANES), f32),
            pltpu.VMEM((CX, STRIDE, LANES), f32),
            pltpu.VMEM((H, LEV, LANES), f32),
            pltpu.VMEM((3, CX, ROWS, LANES), f32),
            pltpu.VMEM((3, CHUNKS, 2, ROWS, LANES), f32),
            pltpu.VMEM((3, CHUNKS, 2, ROWS, LANES), f32),
            pltpu.VMEM((3, CHUNKS, 2, ROWS, LANES), f32),
            pltpu.VMEM((3, CHUNKS, 2, ROWS, LANES), f32),
            pltpu.VMEM((2, ROWS, LANES), f32),
            pltpu.VMEM((2, ROWS, LANES), f32),
            pltpu.VMEM((CX, LANES), f32),
            pltpu.VMEM((2 * LANES, 4 * LANES), jnp.bfloat16),
            pltpu.VMEM((CX * NSC * ROWS, 2 * LANES), jnp.bfloat16),
            pltpu.VMEM((CX * NSC * ROWS, 4 * LANES), f32),
            dma((NSC, CX)),
            dma((2, CX)),
            dma(()),
            dma((3, CHUNKS, 2)),
            dma((3, CHUNKS, 2)),
            dma((3, CHUNKS, 2)),
            dma((3, CHUNKS, 2)),
            dma((2,)),
            dma((2,)),
            dma((2,)),
            dma((2,)),
            pltpu.VMEM((1, slots), i32),
            pltpu.VMEM((1, slots), i32),
            pltpu.VMEM(table.shape, f32),
            pltpu.VMEM((NWL, slots), f32),
            pltpu.VMEM((1, slots), f32),
            pltpu.VMEM((CX, LOW, slots), f32),
            pltpu.VMEM((LOW, slots), f32),
            dma((5,)),
        ],
        compiler_params=pltpu.CompilerParams(collective_id=0, has_side_effects=True, vmem_limit_bytes=32 << 20),
        name="advance",
    )(*operands)


def store_kernel(adv, wall, indoor, out, wall_out, indoor_out, sem, sem_wall, sem_indoor):
    copies = [
        pltpu.make_async_copy(adv.at[x, s], out.at[s, :, x, :], sem.at[s, x]) for s in range(NSC) for x in range(CX)
    ]
    copies.append(pltpu.make_async_copy(wall, wall_out, sem_wall))
    copies.append(pltpu.make_async_copy(indoor, indoor_out, sem_indoor))
    for copy in copies:
        copy.start()
    for copy in copies:
        copy.wait()


def store(adv, wall, indoor):
    f32 = jnp.float32
    anywhere = pl.BlockSpec(memory_space=pl.ANY)
    dma = pltpu.SemaphoreType.DMA
    return pl.pallas_call(
        store_kernel,
        out_shape=(
            jax.ShapeDtypeStruct((NSC, LEV, CX, LANES), f32),
            jax.ShapeDtypeStruct(wall.shape, f32),
            jax.ShapeDtypeStruct(indoor.shape, f32),
        ),
        in_specs=[anywhere] * 3,
        out_specs=(anywhere,) * 3,
        scratch_shapes=[dma((NSC, CX)), dma(()), dma(())],
        compiler_params=pltpu.CompilerParams(vmem_limit_bytes=4 << 20),
        name="store",
    )(adv, wall, indoor)


def per_device(scalars, winds, map_factor, urban_counts, urban_cols, street_class, area_table, wall_temp, indoor_temp):
    adv, walls, rooms = advance(
        scalars, winds, map_factor, urban_counts, urban_cols, street_class, area_table, wall_temp, indoor_temp
    )
    scalars_out, wall_out, indoor_out = store(adv, walls, rooms)
    return (scalars_out, wall_out, indoor_out.reshape(indoor_temp.shape))


def solution(mesh):
    in_specs = (
        P(None, None, "gx", "gy"),
        P(None, None, "gx", "gy"),
        P("gx", "gy"),
        P(("gx", "gy")),
        P(("gx", "gy")),
        P(("gx", "gy")),
        P(),
        P(None, ("gx", "gy")),
        P(("gx", "gy")),
    )
    out_specs = (P(None, None, "gx", "gy"), P(None, ("gx", "gy")), P(("gx", "gy")))
    return jax.shard_map(per_device, mesh=mesh, in_specs=in_specs, out_specs=out_specs, check_vma=False)
```

profile of v0, /device:TPU:0, one launch (start us, length us, event | category | flops | bytes accessed | tf_op | source)
XLA Modules:
  0.0 47.4 jit_solution(900639707381101195)
XLA Ops:
  1.3 44.2 %advance.1 = (f32[16,4,64,128]{3,2,1,0:T(8,128)S(1)}, f32[10,1024]{1,0:T(8,128)S(1)}, f32[1,1024]{1,0:T(1,128)S(1)}) custom-call(f32[4,64,16,128]{3,2,1,0:T(8,128)} %scal.1, f32[2,64,16,128]{3,2,1,0:T(8,128)} %wind.1, f32[16,128]{1,0:T(8,128)} %mapf.1, s32[1]{0:T(128)S(6)} %copy.12.counts, s32[1,1024]{1,0:T(1,128)} %bitcast.4, s32[1,1024]{1,0:T(1,128)} %bitcast.5, ...), custom_call_target="tpu_custom_call" | custom-call | tf_op jit(solution)/shard_map/advance/pallas_call | solution.py:422
  45.5 1.9 %store.1 = (f32[4,64,16,128]{3,2,1,0:T(8,128)}, f32[10,1024]{1,0:T(8,128)}, f32[1,1024]{1,0:T(1,128)}) custom-call(f32[16,4,64,128]{3,2,1,0:T(8,128)S(1)} %get-tuple-element.9.adv, f32[10,1024]{1,0:T(8,128)S(1)} %get-tuple-element.10.wall, f32[1,1024]{1,0:T(1,128)S(1)} %get-tuple-element.11.indoor), custom_call_target="tpu_custom_call" | custom-call | tf_op jit(solution)/shard_map/store/pallas_call | solution.py:493
where the time goes:
time: 47.6 us; the launch traced here: 47.4 us
  Pallas kernels  46.1 us (97%)
  between operations  1.29 us (3%)
    pallas_call x1, Pallas kernels, advance(): pl.pallas_call(step_kernel, out_shape=(jax.ShapeDtypeStruct((CX, NSC, LEV...  44.2 us
    pallas_call x1, Pallas kernels, store(): pl.pallas_call(store_kernel, out_shape=(jax.ShapeDtypeStruct((NSC, LEV, C...  1.9 us

commit v1 on v0

--- a/solution.py
+++ b/solution.py
@@ -24,6 +24,7 @@
 ROWS = 8
 CHUNKS = LEV // ROWS
 STRIDE = LEV + ROWS
+FIRST = 2
 H = 3
 EDGE_X = (0, 1, 2, 13, 14, 15)
 INNER_X = tuple(range(3, 13))
@@ -188,8 +189,7 @@
             copy.start()
         return carry
 
-    lax.fori_loop(0, CHUNKS, send_first, 0)
-    fill_stencil(stencil)
+    lax.fori_loop(0, FIRST, send_first, 0)
 
     lane = lax.broadcasted_iota(jnp.int32, (ROWS, LANES), 1)
     slot = lane // 8
@@ -234,9 +234,15 @@
             pack_send(0, k, pair, packed[at : at + ROWS], packed[at + ROWS : at + 2 * ROWS])
         for copy in y_copies(0, k):
             copy.start()
+
+        @pl.when(k >= FIRST)
+        def _():
+            send_first(k, carry)
+
         return carry
 
     lax.fori_loop(0, CHUNKS, pack_first, 0)
+    fill_stencil(stencil)
 
     load_map.wait()
     for x in range(CX):
@@ -376,7 +382,7 @@
             for copy in x_copies(sec, k) + y_copies(sec, k):
                 copy.wait_recv()
             section(sec, k, False)
-            for copy in x_copies(sec + 1, k) + y_copies(sec + 1, k):
+            for copy in y_copies(sec + 1, k) + x_copies(sec + 1, k):
                 copy.start()
             return carry
 

time: 47.6 us -> 45 us (0.945)
  Pallas kernels: 46.1 us -> 43.5 us
    pallas_call x1, Pallas kernels: 44.2 us -> 41.6 us  [advance(): pl.pallas_call(step_kernel, out_shape=(jax.ShapeDtypeStruct((CX, NSC, LEV...]
where the time goes in v1:
time: 45 us; the launch traced here: 44.8 us
  Pallas kernels  43.5 us (97%)
  between operations  1.29 us (3%)
    pallas_call x1, Pallas kernels, advance(): pl.pallas_call(step_kernel, out_shape=(jax.ShapeDtypeStruct((CX, NSC, LEV...  41.6 us
    pallas_call x1, Pallas kernels, store(): pl.pallas_call(store_kernel, out_shape=(jax.ShapeDtypeStruct((NSC, LEV, C...  1.9 us

profile of v1, /device:TPU:0, one launch (start us, length us, event | category | flops | bytes accessed | tf_op | source)
XLA Modules:
  0.0 44.8 jit_solution(15213103914147795415)
XLA Ops:
  1.3 41.6 %advance.1 = (f32[16,4,64,128]{3,2,1,0:T(8,128)S(1)}, f32[10,1024]{1,0:T(8,128)S(1)}, f32[1,1024]{1,0:T(1,128)S(1)}) custom-call(f32[4,64,16,128]{3,2,1,0:T(8,128)} %scal.1, f32[2,64,16,128]{3,2,1,0:T(8,128)} %wind.1, f32[16,128]{1,0:T(8,128)} %mapf.1, s32[1]{0:T(128)S(6)} %copy.12.counts, s32[1,1024]{1,0:T(1,128)} %bitcast.4, s32[1,1024]{1,0:T(1,128)} %bitcast.5, ...), custom_call_target="tpu_custom_call" | custom-call | tf_op jit(solution)/shard_map/advance/pallas_call | solution.py:428
  42.9 1.9 %store.1 = (f32[4,64,16,128]{3,2,1,0:T(8,128)}, f32[10,1024]{1,0:T(8,128)}, f32[1,1024]{1,0:T(1,128)}) custom-call(f32[16,4,64,128]{3,2,1,0:T(8,128)S(1)} %get-tuple-element.9.adv, f32[10,1024]{1,0:T(8,128)S(1)} %get-tuple-element.10.wall, f32[1,1024]{1,0:T(1,128)S(1)} %get-tuple-element.11.indoor), custom_call_target="tpu_custom_call" | custom-call | tf_op jit(solution)/shard_map/store/pallas_call | solution.py:499

commit v2 on v1

--- a/solution.py
+++ b/solution.py
@@ -113,24 +113,22 @@
     for device in (east, west, north, south):
         pl.semaphore_signal(barrier, inc=1, device_id=device, device_id_type=MESH)
 
-    def load_scalar(s, x):
-        return pltpu.make_async_copy(scal.at[s, :, x, :], field0.at[H + x, s, pl.ds(0, LEV), :], load_s.at[s, x])
+    def load_scalar(x):
+        return pltpu.make_async_copy(scal.at[:, :, x, :], field0.at[H + x, :, pl.ds(0, LEV), :], load_s.at[x])
 
     def load_wind(which, x):
         target = (windx.at[1 + x] if which == 0 else windy.at[x]).at[pl.ds(0, LEV), :]
         return pltpu.make_async_copy(wind.at[which, :, x, :], target, load_w.at[which, x])
 
     load_map = pltpu.make_async_copy(mapf, mapbuf, load_m)
-    for s in range(NSC):
-        for x in EDGE_X:
-            load_scalar(s, x).start()
+    for x in EDGE_X:
+        load_scalar(x).start()
     load_wind(0, 0).start()
     load_wind(0, CX - 1).start()
     for x in range(CX):
         load_wind(1, x).start()
-    for s in range(NSC):
-        for x in INNER_X:
-            load_scalar(s, x).start()
+    for x in INNER_X:
+        load_scalar(x).start()
     for x in range(1, CX - 1):
         load_wind(0, x).start()
     load_map.start()
@@ -175,9 +173,8 @@
         remote(wpack.at[1], wgot.at[1], swy.at[1], rwy.at[1], south),
     )
 
-    for s in range(NSC):
-        for x in EDGE_X:
-            load_scalar(s, x).wait()
+    for x in EDGE_X:
+        load_scalar(x).wait()
     load_wind(0, 0).wait()
     load_wind(0, CX - 1).wait()
     pl.semaphore_wait(barrier, 4)
@@ -217,9 +214,8 @@
     for copy in wy_copies:
         copy.start()
 
-    for s in range(NSC):
-        for x in INNER_X:
-            load_scalar(s, x).wait()
+    for x in INNER_X:
+        load_scalar(x).wait()
 
     many = lax.broadcasted_iota(jnp.int32, (NSC * ROWS, LANES), 1) // 8
 
@@ -455,7 +451,7 @@
             pltpu.VMEM((2 * LANES, 4 * LANES), jnp.bfloat16),
             pltpu.VMEM((CX * NSC * ROWS, 2 * LANES), jnp.bfloat16),
             pltpu.VMEM((CX * NSC * ROWS, 4 * LANES), f32),
-            dma((NSC, CX)),
+            dma((CX,)),
             dma((2, CX)),
             dma(()),
             dma((3, CHUNKS, 2)),
@@ -482,7 +478,7 @@
 
 def store_kernel(adv, wall, indoor, out, wall_out, indoor_out, sem, sem_wall, sem_indoor):
     copies = [
-        pltpu.make_async_copy(adv.at[x, s], out.at[s, :, x, :], sem.at[s, x]) for s in range(NSC) for x in range(CX)
+        pltpu.make_async_copy(adv.at[x], out.at[:, :, x, :], sem.at[x]) for x in range(CX)
     ]
     copies.append(pltpu.make_async_copy(wall, wall_out, sem_wall))
     copies.append(pltpu.make_async_copy(indoor, indoor_out, sem_indoor))
@@ -505,7 +501,7 @@
         ),
         in_specs=[anywhere] * 3,
         out_specs=(anywhere,) * 3,
-        scratch_shapes=[dma((NSC, CX)), dma(()), dma(())],
+        scratch_shapes=[dma((CX,)), dma(()), dma(())],
         compiler_params=pltpu.CompilerParams(vmem_limit_bytes=4 << 20),
         name="store",
     )(adv, wall, indoor)

time: 45 us -> 44.1 us (0.980)
  Pallas kernels: 43.5 us -> 42.7 us
where the time goes in v2:
time: 44.1 us; the launch traced here: 44 us
  Pallas kernels  42.7 us (97%)
  between operations  1.29 us (3%)
    pallas_call x1, Pallas kernels, advance(): pl.pallas_call(step_kernel, out_shape=(jax.ShapeDtypeStruct((CX, NSC, LEV...  41.2 us
    pallas_call x1, Pallas kernels, store(): pl.pallas_call(store_kernel, out_shape=(jax.ShapeDtypeStruct((NSC, LEV, C...  1.48 us

profile of v2, /device:TPU:0, one launch (start us, length us, event | category | flops | bytes accessed | tf_op | source)
XLA Modules:
  0.0 44.0 jit_solution(3222036352993847379)
XLA Ops:
  1.3 41.2 %advance.1 = (f32[16,4,64,128]{3,2,1,0:T(8,128)S(1)}, f32[10,1024]{1,0:T(8,128)S(1)}, f32[1,1024]{1,0:T(1,128)S(1)}) custom-call(f32[4,64,16,128]{3,2,1,0:T(8,128)} %scal.1, f32[2,64,16,128]{3,2,1,0:T(8,128)} %wind.1, f32[16,128]{1,0:T(8,128)} %mapf.1, s32[1]{0:T(128)S(6)} %copy.12.counts, s32[1,1024]{1,0:T(1,128)} %bitcast.4, s32[1,1024]{1,0:T(1,128)} %bitcast.5, ...), custom_call_target="tpu_custom_call" | custom-call | tf_op jit(solution)/shard_map/advance/pallas_call | solution.py:424
  42.5 1.5 %store.1 = (f32[4,64,16,128]{3,2,1,0:T(8,128)}, f32[10,1024]{1,0:T(8,128)}, f32[1,1024]{1,0:T(1,128)}) custom-call(f32[16,4,64,128]{3,2,1,0:T(8,128)S(1)} %get-tuple-element.9.adv, f32[10,1024]{1,0:T(8,128)S(1)} %get-tuple-element.10.wall, f32[1,1024]{1,0:T(1,128)S(1)} %get-tuple-element.11.indoor), custom_call_target="tpu_custom_call" | custom-call | tf_op jit(solution)/shard_map/store/pallas_call | solution.py:495

commit v3 on v2

--- a/solution.py
+++ b/solution.py
@@ -260,7 +260,8 @@
     lanes = lax.broadcasted_iota(jnp.int32, (half_levels, LANES), 1)
     slots, within = lanes // 8, lanes % 8
     below = within < 3
-    for part in range(2):
+
+    def prepare(part):
         rows = pl.ds(part * half_levels, half_levels)
         for x in range(CX + 1):
             facex[x, rows, :] = (windx[x, rows, :] + windx[x + 1, rows, :]) * (1.0 / 120.0)
@@ -305,6 +306,7 @@
         edge_weight[1, rows, :] = two
         edge_weight[2, rows, :] = three
 
+    prepare(0)
     size = NSC * ROWS
     half = CX // 2
     edge = (lane < H) | (lane >= LANES - H)
@@ -375,6 +377,12 @@
     for sec in range(2):
 
         def early(k, carry, sec=sec):
+            if sec == 0:
+
+                @pl.when(k == CHUNKS // 2)
+                def _():
+                    prepare(1)
+
             for copy in x_copies(sec, k) + y_copies(sec, k):
                 copy.wait_recv()
             section(sec, k, False)
@@ -385,6 +393,9 @@
         lax.fori_loop(0, CHUNKS, early, 0)
 
     def late(k, carry):
+        for sec in range(2):
+            for copy in x_copies(sec, k) + y_copies(sec, k):
+                copy.wait_send()
         for copy in x_copies(2, k) + y_copies(2, k):
             copy.wait_recv()
         section(2, k, True)
@@ -403,9 +414,8 @@
         copy.wait_send()
 
     def finish(k, carry):
-        for sec in range(3):
-            for copy in x_copies(sec, k) + y_copies(sec, k):
-                copy.wait_send()
+        for copy in x_copies(2, k) + y_copies(2, k):
+            copy.wait_send()
         return carry
 
     lax.fori_loop(0, CHUNKS, finish, 0)

time: 44.1 us -> 44 us (level)
  no operation moved by 1% of the time
where the time goes in v3:
time: 44 us; the launch traced here: 43.9 us
  Pallas kernels  42.6 us (97%)
  between operations  1.29 us (3%)
    pallas_call x1, Pallas kernels, advance(): pl.pallas_call(step_kernel, out_shape=(jax.ShapeDtypeStruct((CX, NSC, LEV...  41.1 us
    pallas_call x1, Pallas kernels, store(): pl.pallas_call(store_kernel, out_shape=(jax.ShapeDtypeStruct((NSC, LEV, C...  1.48 us

profile of v3, /device:TPU:0, one launch (start us, length us, event | category | flops | bytes accessed | tf_op | source)
XLA Modules:
  0.0 43.9 jit_solution(11656026959733764900)
XLA Ops:
  1.3 41.1 %advance.1 = (f32[16,4,64,128]{3,2,1,0:T(8,128)S(1)}, f32[10,1024]{1,0:T(8,128)S(1)}, f32[1,1024]{1,0:T(1,128)S(1)}) custom-call(f32[4,64,16,128]{3,2,1,0:T(8,128)} %scal.1, f32[2,64,16,128]{3,2,1,0:T(8,128)} %wind.1, f32[16,128]{1,0:T(8,128)} %mapf.1, s32[1]{0:T(128)S(6)} %copy.12.counts, s32[1,1024]{1,0:T(1,128)} %bitcast.4, s32[1,1024]{1,0:T(1,128)} %bitcast.5, ...), custom_call_target="tpu_custom_call" | custom-call | tf_op jit(solution)/shard_map/advance/pallas_call | solution.py:434
  42.4 1.5 %store.1 = (f32[4,64,16,128]{3,2,1,0:T(8,128)}, f32[10,1024]{1,0:T(8,128)}, f32[1,1024]{1,0:T(1,128)}) custom-call(f32[16,4,64,128]{3,2,1,0:T(8,128)S(1)} %get-tuple-element.9.adv, f32[10,1024]{1,0:T(8,128)S(1)} %get-tuple-element.10.wall, f32[1,1024]{1,0:T(1,128)S(1)} %get-tuple-element.11.indoor), custom_call_target="tpu_custom_call" | custom-call | tf_op jit(solution)/shard_map/store/pallas_call | solution.py:505
